TPU v7x, 32 devices: a whole 2x2x4 slice. The times are simulated.
32 devices in a mesh: row: 4 (over y, core), col: 8 (over z, x).
Axes of the slice: x: 2, y: 2, z: 4, core: 2. Of those that a mesh axis runs over, the one named last changes fastest.
Arguments:
- image: bfloat16 [1024, 1024], P(('col', 'row')), may hold values from -1 to 1
- text: bfloat16 [1024, 1024], P(('row', 'col')), may hold values from -1 to 1
- audio: bfloat16 [1024, 1024], P(('row', 'col')), may hold values from -1 to 1
Outputs:
- image_grad: float32 [1024, 1024], P(('col', 'row'))
- text_grad: float32 [1024, 1024], P(('row', 'col'))
- audio_grad: float32 [1024, 1024], P(('row', 'col'))
- loss: float32 [], replicated
All inputs are finite; a program needn't handle non-finite values.
Results may differ from a plain program's by a relative error of at most 0.0063.
Values may be sent and summed in bfloat16 or wider, within the bound.
A program may use at most 64 MiB of HBM per device.

v0:
```python
import jax
import jax.numpy as jnp
from jax import lax
from jax.sharding import PartitionSpec as P

logit_scale = 20.0
epsilon = 1e-06


def normalize(values):
    widened = values.astype(jnp.float32)
    radius = jnp.sqrt(jnp.sum(widened * widened, axis=-1, keepdims=True) + epsilon)
    return (widened / radius, radius)


def through_norm(grad_unit, unit, radius):
    inner = jnp.sum(unit * grad_unit, axis=-1, keepdims=True)
    return (grad_unit - unit * inner) / radius


def scores(left, right):
    return logit_scale * lax.dot_general(
        left, right, (((1,), (1,)), ((), ())), preferred_element_type=jnp.float32
    )


def contract_rows(weights_part, image_tile):
    return lax.dot_general(
        weights_part, image_tile, (((0,), (0,)), ((), ())), preferred_element_type=jnp.float32
    )


def pair_scores(image_tile, text_tile, audio_tile):
    text_scores = scores(image_tile, text_tile)
    audio_scores = scores(image_tile, audio_tile)
    return (
        text_scores,
        audio_scores,
        jnp.exp(text_scores - logit_scale),
        jnp.exp(audio_scores - logit_scale),
    )


def softmax_weights(exp_tile, row_total, column_total, twice_diagonal):
    return (
        exp_tile / row_total[:, None] + exp_tile / column_total[None, :] - twice_diagonal
    ).astype(jnp.bfloat16)


def own_logs(totals, first_row, amount):
    return jnp.sum(jnp.log(lax.dynamic_slice_in_dim(totals, first_row, amount, 0)))


def shards(image, text, audio):
    rows_here = image.shape[0]
    feature_width = image.shape[1]
    image_unit, image_radius = normalize(image)
    text_unit, text_radius = normalize(text)
    audio_unit, audio_radius = normalize(audio)
    image_half = image_unit.astype(jnp.bfloat16)
    text_half = text_unit.astype(jnp.bfloat16)
    audio_half = audio_unit.astype(jnp.bfloat16)
    row_place = lax.axis_index("row")
    col_place = lax.axis_index("col")
    row_count = lax.axis_size("row")
    col_count = lax.axis_size("col")
    image_tile = lax.all_gather(image_half, "col", axis=0, tiled=True)
    text_tile, audio_tile = (
        lax.all_gather(text_half, "row", axis=0, tiled=True),
        lax.all_gather(audio_half, "row", axis=0, tiled=True),
    )
    image_local = jnp.arange(col_count * rows_here, dtype=jnp.int32)
    image_ids = (
        image_local // rows_here * row_count + row_place
    ) * rows_here + image_local % rows_here
    pair_local = jnp.arange(row_count * rows_here, dtype=jnp.int32)
    pair_ids = (
        pair_local // rows_here * col_count + col_place
    ) * rows_here + pair_local % rows_here
    text_scores, audio_scores, text_exp, audio_exp = pair_scores(image_tile, text_tile, audio_tile)
    text_row, audio_row = lax.psum((jnp.sum(text_exp, axis=1), jnp.sum(audio_exp, axis=1)), "col")
    text_column, audio_column = lax.psum(
        (jnp.sum(text_exp, axis=0), jnp.sum(audio_exp, axis=0)), "row"
    )
    diagonal = image_ids[:, None] == pair_ids[None, :]
    twice_diagonal = jnp.where(diagonal, 2.0, 0.0).astype(jnp.float32)
    text_weights = softmax_weights(text_exp, text_row, text_column, twice_diagonal)
    audio_weights = softmax_weights(audio_exp, audio_row, audio_column, twice_diagonal)
    image_part = logit_scale * lax.psum_scatter(
        jnp.dot(text_weights, text_tile, preferred_element_type=jnp.float32)
        + jnp.dot(audio_weights, audio_tile, preferred_element_type=jnp.float32),
        "col",
        scatter_dimension=0,
        tiled=True,
    )
    partial_value = jnp.concatenate(
        [contract_rows(text_weights, image_tile), contract_rows(audio_weights, image_tile)], axis=1
    )
    pair_part = logit_scale * lax.psum_scatter(
        partial_value, "row", scatter_dimension=0, tiled=True
    )
    image_first = col_place * rows_here
    pair_first = row_place * rows_here
    loss_part = (
        own_logs(text_row, image_first, rows_here)
        + own_logs(audio_row, image_first, rows_here)
        + own_logs(text_column, pair_first, rows_here)
        + own_logs(audio_column, pair_first, rows_here)
        - 2.0 * jnp.sum(jnp.where(diagonal, text_scores + audio_scores, 0.0))
    )
    batch_size = rows_here * row_count * col_count
    loss = lax.psum(loss_part, ("row", "col")) / (4.0 * batch_size) + logit_scale
    return (
        through_norm(image_part, image_unit, image_radius),
        through_norm(pair_part[:, :feature_width], text_unit, text_radius),
        through_norm(pair_part[:, feature_width:], audio_unit, audio_radius),
        loss,
    )


def solution(mesh):
    in_specs = (P(("col", "row"), None), P(("row", "col"), None), P(("row", "col"), None))
    out_specs = (P(("col", "row"), None), P(("row", "col"), None), P(("row", "col"), None), P())
    return jax.shard_map(shards, mesh=mesh, in_specs=in_specs, out_specs=out_specs, check_vma=False)
```

profile of v0, /device:TPU:0, one launch (start us, length us, event | category | flops | bytes accessed | tf_op | source)
XLA Modules:
  0.0 184.7 jit_solution(4883369968450899383)
XLA Ops:
  7.2 0.0 copy-start.2
  7.2 0.0 reduce-scatter.5.cloned.1.call-start
  7.2 1.0 fusion.1
  8.2 0.0 copy-done.2
  8.2 0.1 fusion.21
  8.3 0.0 copy-start
  8.3 7.4 %all_gather.10 = bf16[128,1024]{1,0:T(8,128)(2,1)S(1)} all-gather(bf16[32,1024]{1,0:T(8,128)(2,1)S(1)} %fusion.21), channel_id=1, replica_groups=mesh['row'=4,'col'=8] {'row'}, dimensions={0}, use_global_device_ids=true | all-gather | bytes 327680 | tf_op jit(solution)/shard_map/all_gather | solution.py:69
  15.7 0.0 copy-done
  15.7 0.1 fusion
  15.8 0.1 fusion.20
  15.9 0.0 copy-start.1
  15.9 32.0 %all_gather.9 = bf16[256,1024]{1,0:T(8,128)(2,1)S(1)} all-gather(bf16[32,1024]{1,0:T(8,128)(2,1)S(1)} %fusion.20), channel_id=1, replica_groups=mesh['row'=4,'col'=8] {'col'}, dimensions={0}, use_global_device_ids=true | all-gather | bytes 589824 | tf_op jit(solution)/shard_map/all_gather | solution.py:67
  47.9 0.0 copy-done.1
  47.9 0.1 fusion.2
  48.1 0.1 fusion.22
  48.2 5.8 %all_gather.11 = bf16[128,1024]{1,0:T(8,128)(2,1)S(1)} all-gather(bf16[32,1024]{1,0:T(8,128)(2,1)S(1)} %fusion.22), channel_id=1, replica_groups=mesh['row'=4,'col'=8] {'row'}, dimensions={0}, use_global_device_ids=true | all-gather | bytes 327680 | tf_op jit(solution)/shard_map/all_gather | solution.py:70
  54.0 0.3 convolution_multiply_fusion
  54.3 0.9 fusion.3
  55.2 7.1 %all-reduce.1 = (f32[128]{0:T(128)S(1)}, f32[128]{0:T(128)S(1)}) all-reduce(f32[128]{0:T(128)S(1)} %get-tuple-element.9, f32[128]{0:T(128)S(1)} %get-tuple-element.7), channel_id=1, replica_groups=mesh['row'=4,'col'=8] {'row'}, use_global_device_ids=true, to_apply=%region_5.6 | all-reduce | flops 256 | bytes 2048 | tf_op jit(solution)/shard_map/psum | solution.py:82
  62.3 21.2 %all-reduce = (f32[256]{0:T(256)S(1)}, f32[256]{0:T(256)S(1)}) all-reduce(f32[256]{0:T(256)S(1)} %get-tuple-element.10, f32[256]{0:T(256)S(1)} %get-tuple-element.8), channel_id=1, replica_groups=mesh['row'=4,'col'=8] {'col'}, use_global_device_ids=true, to_apply=%region_3.4 | all-reduce | flops 512 | bytes 4096 | tf_op jit(solution)/shard_map/psum | solution.py:81
  83.5 0.4 fusion.23
  83.9 0.4 fusion.26
  84.2 1.1 pad_maximum_fusion
  85.4 0.0 reduce-scatter.5.cloned.1.call-update
  85.4 0.0 reduce-scatter.3.cloned.1.call-start
  85.4 0.4 fusion.28
  85.8 1.4 convolution_add_fusion
  87.1 0.0 reduce-scatter.3.cloned.1.call-update
  87.2 0.7 log_reduce_fusion.2
  89.2 0.7 log_reduce_fusion
  91.8 37.1 %psum.39 = f32[]{:T(128)} all-reduce(f32[]{:T(128)S(6)} %sub.45), channel_id=1, replica_groups=mesh['row'=4,'col'=8] {'row','col'}, use_global_device_ids=true, to_apply=%region_21.22 | all-reduce | flops 1 | bytes 8 | tf_op jit(solution)/shard_map/psum | solution.py:112
  129.6 0.0 reduce-scatter.5.cloned.1.call-done
  129.6 1.0 broadcast_multiply_fusion
  130.6 0.2 multiply_reduce_fusion
  130.8 0.8 subtract_divide_fusion
  131.6 43.1 %reduce-scatter.3.cloned.1.call-done = f32[32,1024]{1,0:T(8,128)} async-done(((f32[256,1024]{1,0:T(8,128)}), f32[32,1024]{1,0:T(8,128)}) %reduce-scatter.3.cloned.1.call-update) | async-done | bytes 131088 | tf_op jit(solution)/shard_map/reduce_scatter | solution.py:89
  174.8 0.0 copy-start.3
  174.8 1.2 multiply_reduce_fusion.2
  175.9 0.0 copy-done.3
  175.9 0.8 subtract_divide_fusion.2
  (5 shorter events, 0.0 us)
Async XLA Ops:
  7.2 1.0 copy-start.2
  7.2 122.4 %reduce-scatter.5.cloned.1.call-start = ((), (), s32[]{:S(2)}) async-start(), calls=%async_computation.3 | async-start | bytes 1310720 | tf_op jit(solution)/shard_map/reduce_scatter | solution.py:99
  8.3 7.4 %copy-start = (bf16[32,1024]{1,0:T(8,128)(2,1)S(1)}, bf16[32,1024]{1,0:T(8,128)(2,1)}, u32[]{:S(2)}) copy-start(bf16[32,1024]{1,0:T(8,128)(2,1)} %param.3) | copy-start | bytes 196612
  15.9 32.0 %copy-start.1 = (bf16[32,1024]{1,0:T(8,128)(2,1)S(1)}, bf16[32,1024]{1,0:T(8,128)(2,1)}, u32[]{:S(2)}) copy-start(bf16[32,1024]{1,0:T(8,128)(2,1)} %param.5) | copy-start | bytes 196612
  85.4 89.4 %reduce-scatter.3.cloned.1.call-start = ((), (), s32[]{:S(2)}) async-start(), calls=%async_computation.2 | async-start | bytes 1179648 | tf_op jit(solution)/shard_map/reduce_scatter | solution.py:89
  174.8 1.2 copy-start.3
Sparse Core Ops, SparseCore 0:
  85.5 21.2 reduce-scatter.4
  110.2 64.5 reduce-scatter.2
where the time goes:
time: 185 us
  blocking collectives  111 us (60%)
  waiting for transfers between devices  43.2 us (23%)
  between operations  19.2 us (10%)
  other arithmetic  7.92 us (4%)
  matrix products  3.67 us (2%)
    reduce_scatter x1, waiting for transfers between devices, shards(): lax.psum_scatter(jnp.dot(text_weights, text_tile, preferred_element_type=...  43.1 us
    psum x1, blocking collectives, shards(): lax.psum(loss_part, ('row', 'col')) / (4.0 * batch_size) + logit_scale  37.1 us
    all_gather x1, blocking collectives, shards(): image_tile = lax.all_gather(image_half, 'col', axis=0, tiled=True)  32 us
    psum x1, blocking collectives, shards(): lax.psum((jnp.sum(text_exp, axis=1), jnp.sum(audio_exp, axis=1)), 'col')  21.2 us
    all_gather x1, blocking collectives, shards(): lax.all_gather(text_half, 'row', axis=0, tiled=True)  7.38 us
    psum x1, blocking collectives, shards(): lax.psum((jnp.sum(text_exp, axis=0), jnp.sum(audio_exp, axis=0)), 'row')  7.09 us
    all_gather x1, blocking collectives, shards(): lax.all_gather(audio_half, 'row', axis=0, tiled=True)  5.78 us
  transfers between devices with their start and end apart: 2, of which 1 were waited for; matrix products, arithmetic and copies ran while one was open for 3% of the time, Pallas kernels for 0%

commit v1 on v0

v1 whole, which is shorter than its diff:
```python
import functools

import jax
import jax.numpy as jnp
from jax import lax
from jax.experimental import pallas as pl
from jax.experimental.pallas import tpu as pltpu
from jax.sharding import PartitionSpec as P

MESH = pl.DeviceIdType.MESH
logit_scale = 20.0
epsilon = 1e-06


def inverse_radius(values):
    return lax.rsqrt(jnp.sum(values * values, axis=-1, keepdims=True) + epsilon)


def contract(left, right, left_dim, right_dim):
    return lax.dot_general(
        left, right, (((left_dim,), (right_dim,)), ((), ())), preferred_element_type=jnp.float32
    )


def loop(count, body):
    if count == 1:
        body(0)
    else:

        def step(index, carry):
            body(index)
            return carry

        lax.fori_loop(0, count, step, 0)


def kernel(
    R, C, n, F, G,
    image_ref, text_ref, audio_ref,
    image_out, text_out, audio_out, loss_out,
    img, pair, exp_ip, exp_pi, stat_c, stat_r, loss_c, loss_r,
    part_i, recv_i, part_p, recv_p, acc,
    img_s, img_r, pair_s, pair_r, sc_s, sc_r, sr_s, sr_r,
    lc_s, lc_r, lr_s, lr_r, pi_s, pi_r, pp_s, pp_r,
):
    r = lax.axis_index("row")
    c = lax.axis_index("col")
    B = C // G
    M = B * n
    H = R * n
    Q = 2 * H
    cols = [lax.rem(c + k, C) for k in range(1, C)]
    rows = [lax.rem(r + k, R) for k in range(1, R)]

    barrier = pltpu.get_barrier_semaphore()
    for p in cols:
        pl.semaphore_signal(barrier, inc=1, device_id=(r, p), device_id_type=MESH)
    for p in rows:
        pl.semaphore_signal(barrier, inc=1, device_id=(p, c), device_id_type=MESH)

    def to_col(src, dst, send, recv, p):
        return pltpu.make_async_remote_copy(
            src_ref=src, dst_ref=dst, send_sem=send.at[p], recv_sem=recv.at[c],
            device_id=(r, p), device_id_type=MESH,
        )

    def to_row(src, dst, send, recv, p):
        return pltpu.make_async_remote_copy(
            src_ref=src, dst_ref=dst, send_sem=send.at[p], recv_sem=recv.at[r],
            device_id=(p, c), device_id_type=MESH,
        )

    def from_col(dst, send, recv, p):
        pltpu.make_async_remote_copy(
            src_ref=dst, dst_ref=dst, send_sem=send.at[p], recv_sem=recv.at[p],
            device_id=(r, p), device_id_type=MESH,
        ).wait_recv()

    def from_row(dst, send, recv, p):
        pltpu.make_async_remote_copy(
            src_ref=dst, dst_ref=dst, send_sem=send.at[p], recv_sem=recv.at[p],
            device_id=(p, c), device_id_type=MESH,
        ).wait_recv()

    sent = []

    def go(copy):
        copy.start()
        sent.append(copy)

    x = image_ref[...].astype(jnp.float32)
    img[c] = (x * inverse_radius(x)).astype(jnp.bfloat16)
    x = text_ref[...].astype(jnp.float32)
    pair[0, r] = (x * inverse_radius(x)).astype(jnp.bfloat16)
    x = audio_ref[...].astype(jnp.float32)
    pair[1, r] = (x * inverse_radius(x)).astype(jnp.bfloat16)

    pl.semaphore_wait(barrier, C - 1 + R - 1)
    for p in rows:
        go(to_row(pair.at[:, r], pair.at[:, r], pair_s, pair_r, p))
    for p in cols:
        go(to_col(img.at[c], img.at[c], img_s, img_r, p))
    for p in rows:
        from_row(pair.at[:, p], pair_s, pair_r, p)
    for p in cols:
        from_col(img.at[p], img_s, img_r, p)

    def block_ids(count, shape, axis, stride, first):
        local = lax.broadcasted_iota(jnp.int32, shape, axis)
        return (lax.rem(lax.div(local, n), count) * stride + first) * n + lax.rem(local, n)

    col_sum = jnp.zeros((1, Q), jnp.float32)

    def exps(g):
        images = img[pl.ds(g * B, B)].reshape(M, F)
        pairs = pair[...].reshape(Q, F)
        s_pi = logit_scale * contract(pairs, images, 1, 1)
        image_id = block_ids(B, (1, M), 1, R, r + g * (B * R))
        pair_id = block_ids(R, (Q, 1), 0, C, c)
        diagonal = jnp.sum(jnp.where(image_id == pair_id, s_pi, 0.0), axis=0, keepdims=True)
        e_pi = jnp.exp(s_pi - logit_scale)
        exp_pi[g] = e_pi
        text_row = jnp.sum(e_pi[:H], axis=0, keepdims=True)
        audio_row = jnp.sum(e_pi[H:], axis=0, keepdims=True)
        line = lax.broadcasted_iota(jnp.int32, (8, M), 0)
        stat_c[c, g] = jnp.where(
            line == 0, text_row, jnp.where(line == 1, audio_row, diagonal)
        )
        e_ip = jnp.exp(logit_scale * contract(images, pairs, 1, 1) - logit_scale)
        exp_ip[g] = e_ip
        column = jnp.broadcast_to(jnp.sum(e_ip, axis=0, keepdims=True), (8, Q))
        if G == 1:
            stat_r[r] = column
        else:
            stat_r[r] = jnp.where(g == 0, column, stat_r[r] + column)

    if G > 1:
        stat_r[r] = jnp.zeros((8, Q), jnp.float32)
    loop(G, exps)
    for p in cols:
        go(to_col(stat_c.at[c], stat_c.at[c], sc_s, sc_r, p))
    for p in rows:
        go(to_row(stat_r.at[r], stat_r.at[r], sr_s, sr_r, p))
    for p in rows:
        from_row(stat_r.at[p], sr_s, sr_r, p)
    for p in cols:
        from_col(stat_c.at[p], sc_s, sc_r, p)

    columns = stat_r[0]
    for p in range(1, R):
        columns = columns + stat_r[p]
    columns = columns[0:1]
    inverse_c = 1.0 / columns
    inverse_c_tall = jnp.transpose(jnp.broadcast_to(inverse_c, (128, Q)))
    inverse_c_tall = jnp.concatenate([inverse_c_tall] * (M // 128), axis=1)
    loss_c[c] = jnp.broadcast_to(jnp.sum(jnp.log(columns), keepdims=True), (8, 128))

    def weights(g):
        totals = stat_c[0, g]
        for p in range(1, C):
            totals = totals + stat_c[p, g]
        text_row, audio_row, diagonal = totals[0:1], totals[1:2], totals[2:3]
        loss_part = jnp.sum(
            jnp.log(text_row) + jnp.log(audio_row) - 2.0 * diagonal, keepdims=True
        )
        loss_part = jnp.broadcast_to(loss_part, (8, 128))
        if G == 1:
            loss_r[r] = loss_part
        else:
            loss_r[r] = loss_r[r] + loss_part
        inverse_text = jnp.broadcast_to(1.0 / text_row, (H, M))
        inverse_audio = jnp.broadcast_to(1.0 / audio_row, (H, M))
        w_pi = exp_pi[g] * (
            jnp.concatenate([inverse_text, inverse_audio], axis=0) + inverse_c_tall
        )
        same_pi = block_ids(B, (1, M), 1, R, r + g * (B * R)) == block_ids(R, (Q, 1), 0, C, c)
        w_pi = (w_pi - jnp.where(same_pi, 2.0, 0.0)).astype(jnp.bfloat16)
        w_ip = exp_ip[g] * (
            jnp.concatenate([jnp.transpose(inverse_text), jnp.transpose(inverse_audio)], axis=1)
            + inverse_c
        )
        same_ip = block_ids(B, (M, 1), 0, R, r + g * (B * R)) == block_ids(R, (1, Q), 1, C, c)
        w_ip = (w_ip - jnp.where(same_ip, 2.0, 0.0)).astype(jnp.bfloat16)
        pairs = pair[...].reshape(Q, F)
        part_i[pl.ds(g * B, B)] = (
            contract(w_ip, pairs, 1, 0).astype(jnp.bfloat16).reshape(B, n, F)
        )
        images = img[pl.ds(g * B, B)].reshape(M, F)
        product = contract(w_pi, images, 1, 0)
        if G == 1:
            part_p[...] = product.astype(jnp.bfloat16).reshape(2, R, n, F)
        else:
            acc[...] = acc[...] + product

    if G > 1:
        loss_r[r] = jnp.zeros((8, 128), jnp.float32)
        acc[...] = jnp.zeros_like(acc)
    loop(G, weights)
    if G > 1:
        part_p[...] = acc[...].astype(jnp.bfloat16).reshape(2, R, n, F)

    for p in cols:
        go(to_col(part_i.at[p], recv_i.at[c], pi_s, pi_r, p))
    for p in rows:
        go(to_row(part_p.at[:, p], recv_p.at[:, r], pp_s, pp_r, p))
    for p in cols:
        go(to_col(loss_c.at[c], loss_c.at[c], lc_s, lc_r, p))
    for p in rows:
        go(to_row(loss_r.at[r], loss_r.at[r], lr_s, lr_r, p))

    def finish(values_ref, out_ref, gradient):
        values = values_ref[...].astype(jnp.float32)
        inverse = inverse_radius(values)
        unit = values * inverse
        gradient = logit_scale * gradient
        inner = jnp.sum(unit * gradient, axis=-1, keepdims=True)
        out_ref[...] = (gradient - unit * inner) * inverse

    text_sum = part_p[0, r].astype(jnp.float32)
    audio_sum = part_p[1, r].astype(jnp.float32)
    for p in rows:
        from_row(recv_p.at[:, p], pp_s, pp_r, p)
        text_sum = text_sum + recv_p[0, p].astype(jnp.float32)
        audio_sum = audio_sum + recv_p[1, p].astype(jnp.float32)
    finish(text_ref, text_out, text_sum)
    finish(audio_ref, audio_out, audio_sum)
    image_sum = part_i[c].astype(jnp.float32)
    for p in cols:
        from_col(recv_i.at[p], pi_s, pi_r, p)
        image_sum = image_sum + recv_i[p].astype(jnp.float32)
    finish(image_ref, image_out, image_sum)
    for p in cols:
        from_col(loss_c.at[p], lc_s, lc_r, p)
    for p in rows:
        from_row(loss_r.at[p], lr_s, lr_r, p)
    total = loss_c[0]
    for p in range(1, C):
        total = total + loss_c[p]
    for p in range(R):
        total = total + loss_r[p]
    loss_out[0, 0] = jnp.max(total) / (4.0 * n * R * C) + logit_scale
    for copy in sent:
        copy.wait_send()


def solution(mesh):
    R, C = mesh.shape["row"], mesh.shape["col"]

    def shards(image, text, audio):
        n, F = image.shape
        G = max(1, C // 8)
        B = C // G
        M, Q = B * n, 2 * R * n
        vmem = pl.BlockSpec(memory_space=pltpu.VMEM)
        f32, bf16 = jnp.float32, jnp.bfloat16
        grad = jax.ShapeDtypeStruct((n, F), f32)
        sem = pltpu.SemaphoreType.DMA
        sems = []
        for count in (C, R, C, R, C, R, C, R):
            sems += [sem((count,)), sem((count,))]
        image_grad, text_grad, audio_grad, loss = pl.pallas_call(
            functools.partial(kernel, R, C, n, F, G),
            out_shape=(grad, grad, grad, jax.ShapeDtypeStruct((1, 1), f32)),
            in_specs=[vmem] * 3,
            out_specs=(vmem, vmem, vmem, pl.BlockSpec(memory_space=pltpu.SMEM)),
            scratch_shapes=[
                pltpu.VMEM((C, n, F), bf16),
                pltpu.VMEM((2, R, n, F), bf16),
                pltpu.VMEM((G, M, Q), f32),
                pltpu.VMEM((G, Q, M), f32),
                pltpu.VMEM((C, G, 8, M), f32),
                pltpu.VMEM((R, 8, Q), f32),
                pltpu.VMEM((C, 8, 128), f32),
                pltpu.VMEM((R, 8, 128), f32),
                pltpu.VMEM((C, n, F), bf16),
                pltpu.VMEM((C, n, F), bf16),
                pltpu.VMEM((2, R, n, F), bf16),
                pltpu.VMEM((2, R, n, F), bf16),
                pltpu.VMEM((Q, F) if G > 1 else (8, 128), f32),
            ]
            + sems,
            compiler_params=pltpu.CompilerParams(collective_id=0, has_side_effects=True),
        )(image, text, audio)
        return image_grad, text_grad, audio_grad, loss.reshape(())

    first, second = P(("col", "row"), None), P(("row", "col"), None)
    return jax.shard_map(
        shards,
        mesh=mesh,
        in_specs=(first, second, second),
        out_specs=(first, second, second, P()),
        check_vma=False,
    )
```

time: 185 us -> 44.9 us (0.24)
  blocking collectives: 111 us -> 0 us
  waiting for transfers between devices: 43.2 us -> 0 us
  Pallas kernels: 0 us -> 39.1 us
  between operations: 19.2 us -> 2.35 us
  other arithmetic: 7.92 us -> 0 us
  matrix products: 3.67 us -> 0 us
  local copies, waits for them, and re-layouts: 0.02 us -> 3.21 us
    psum x3 -> x0, blocking collectives: 65.4 us -> none  [the longest x1 37.1 us: shards(): lax.psum(loss_part, ('row', 'col')) / (4.0 * batch_size) + logit_scale]
    all_gather x3 -> x0, blocking collectives: 45.2 us -> none  [the longest x1 32 us: shards(): image_tile = lax.all_gather(image_half, 'col', axis=0, tiled=True)]
    reduce_scatter x2 -> x0, waiting for transfers between devices: 43.2 us -> none  [the longest x1 43.1 us: shards(): lax.psum_scatter(jnp.dot(text_weights, text_tile, preferred_element_type=...]
    pallas_call x0 -> x1, Pallas kernels: none -> 39.1 us  [shards(): pl.pallas_call(functools.partial(kernel, R, C, n, F, G), out_shape=(grad,...]
    reduce_sum x7 -> x0, other arithmetic: 3.97 us -> none  [the longest x2 1.39 us: through_norm(): inner = jnp.sum(unit * grad_unit, axis=-1, keepdims=True)]
    dot_general x6 -> x0, matrix products: 3.67 us -> none  [the longest x1 1.35 us: shards(): jnp.dot(audio_weights, audio_tile, preferred_element_type=jnp.float32)]
    unnamed x8 -> x7, local copies, waits for them, and re-layouts: 0.02 us -> 3.21 us
  transfers between devices with their start and end apart: 2 -> 0, of which waited for: 1 -> 0; matrix products, arithmetic and copies ran while one was open for 3% -> 0% of each run, Pallas kernels for 0% -> 0%
where the time goes in v1:
time: 44.9 us; the launch traced here: 44.6 us
  Pallas kernels  39.1 us (87%)
  local copies, waits for them, and re-layouts  3.21 us (7%)
  between operations  2.35 us (5%)
    pallas_call x1, Pallas kernels, shards(): pl.pallas_call(functools.partial(kernel, R, C, n, F, G), out_shape=(grad,...  39.1 us
    unnamed x7, local copies, waits for them, and re-layouts  3.21 us

profile of v1, /device:TPU:0, one launch (start us, length us, event | category | flops | bytes accessed | tf_op | source)
XLA Modules:
  0.0 44.6 jit_solution(797140019343310153)
XLA Ops:
  0.6 39.1 %shard_map.66 = (f32[32,1024]{1,0:T(8,128)}, f32[32,1024]{1,0:T(8,128)}, f32[32,1024]{1,0:T(8,128)}, f32[1,1]{1,0:T(1,128)}) custom-call(bf16[32,1024]{1,0:T(8,128)(2,1)} %image_ref.1, bf16[32,1024]{1,0:T(8,128)(2,1)} %text_ref.1, bf16[32,1024]{1,0:T(8,128)(2,1)} %audio_ref.1), custom_call_target="tpu_custom_call" | custom-call | tf_op jit(solution)/shard_map/pallas_call | solution.py:261
  39.7 0.0 copy-start.1
  39.7 1.6 %copy.11 = f32[32,1024]{1,0:T(8,128)} copy(f32[32,1024]{1,0:T(8,128)} %get-tuple-element.16) | data formatting | bytes 262144
  41.3 0.0 copy-done.1
  41.3 0.0 copy-start
  41.3 0.7 %copy.12 = f32[32,1024]{1,0:T(8,128)} copy(f32[32,1024]{1,0:T(8,128)S(1)} %copy-done.1) | data formatting | bytes 262144
  42.0 0.3 copy-done
  42.3 0.7 %copy.13 = f32[32,1024]{1,0:T(8,128)} copy(f32[32,1024]{1,0:T(8,128)S(1)} %copy-done) | data formatting | bytes 262144
Async XLA Ops:
  39.7 1.6 %copy-start.1 = (f32[32,1024]{1,0:T(8,128)S(1)}, f32[32,1024]{1,0:T(8,128)}, u32[]{:S(2)}) copy-start(f32[32,1024]{1,0:T(8,128)} %get-tuple-element.17) | copy-start | bytes 393220
  41.3 1.0 %copy-start = (f32[32,1024]{1,0:T(8,128)S(1)}, f32[32,1024]{1,0:T(8,128)}, u32[]{:S(2)}) copy-start(f32[32,1024]{1,0:T(8,128)} %get-tuple-element.18) | copy-start | bytes 393220

commit v2 on v0

v2 whole, which is shorter than its diff:
```python
import functools

import jax
import jax.numpy as jnp
from jax import lax
from jax.experimental import pallas as pl
from jax.experimental.pallas import tpu as pltpu
from jax.sharding import PartitionSpec as P

MESH = pl.DeviceIdType.MESH
logit_scale = 20.0
epsilon = 1e-06


def inverse_radius(values):
    return lax.rsqrt(jnp.sum(values * values, axis=-1, keepdims=True) + epsilon)


def contract(left, right, left_dim, right_dim):
    return lax.dot_general(
        left, right, (((left_dim,), (right_dim,)), ((), ())), preferred_element_type=jnp.float32
    )


def kernel(
    R, C, X, n, F,
    image_ref, text_ref, audio_ref,
    image_out, text_out, audio_out, loss_out,
    img, pair, stat_a, stat_b, loss_a, loss_b,
    part_i, recv_i, acc, part_p, recv_h, recv_p,
    img_s, img_r, sa_s, sa_r, la_s, la_r, pi_s, pi_r,
    pair_s, pair_r, sb_s, sb_r, lb_s, lb_r, ph_s, ph_r, pp_s, pp_r, fw_s,
):
    r = lax.axis_index("row")
    c = lax.axis_index("col")
    A, B = C // X, R * X
    M, H = A * n, B * n
    Q = 2 * H
    a = lax.div(c, X)
    x = lax.rem(c, X)
    b = r * X + x
    step = 2 if R % 2 == 0 else 1
    sibling = r + 1 - 2 * lax.rem(r, 2)
    lines = [lax.rem(a + k, A) for k in range(1, A)]
    planes = [lax.rem(b + k, B) for k in range(1, B)]
    turns = [
        (lax.rem(r + i, R), lax.rem(x + j, X))
        for i in range(R - step, -1, -step)
        for j in range(X - 1, -1, -1)
    ]
    mates = [p * X + q for p, q in turns[:-1]]
    crossed = [(p + sibling - r) * X + q for p, q in turns] if step == 2 else []

    def line(p):
        return (r, p * X + x)

    def plane(p):
        return (lax.div(p, X), a * X + lax.rem(p, X))

    def copy(src, dst, send, recv, device):
        return pltpu.make_async_remote_copy(
            src_ref=src, dst_ref=dst, send_sem=send, recv_sem=recv,
            device_id=device, device_id_type=MESH,
        )

    sent = []

    def go(*args):
        one = copy(*args)
        one.start()
        sent.append(one)

    def arrive(dst, send, recv, device):
        copy(dst, dst, send, recv, device).wait_recv()

    barrier = pltpu.get_barrier_semaphore()
    for p in lines[::-1]:
        pl.semaphore_signal(barrier, inc=1, device_id=line(p), device_id_type=MESH)
    for p in planes:
        pl.semaphore_signal(barrier, inc=1, device_id=plane(p), device_id_type=MESH)

    v = image_ref[...].astype(jnp.float32)
    img[a] = (v * inverse_radius(v)).astype(jnp.bfloat16)
    v = text_ref[...].astype(jnp.float32)
    pair[0, b] = (v * inverse_radius(v)).astype(jnp.bfloat16)
    v = audio_ref[...].astype(jnp.float32)
    pair[1, b] = (v * inverse_radius(v)).astype(jnp.bfloat16)

    pl.semaphore_wait(barrier, A - 1 + B - 1)
    for p in mates:
        go(pair.at[:, b], pair.at[:, b], pair_s.at[p], pair_r.at[b], plane(p))
    for p in lines:
        go(img.at[a], img.at[a], img_s.at[p], img_r.at[a], line(p))
    if step == 2:
        go(pair.at[:, b], pair.at[:, b], fw_s.at[b], pair_r.at[b], (sibling, c))
    for p in mates[::-1]:
        arrive(pair.at[:, p], pair_s.at[p], pair_r.at[p], plane(p))
        if step == 2:
            go(pair.at[:, p], pair.at[:, p], fw_s.at[p], pair_r.at[p], (sibling, c))
    for p in lines:
        arrive(img.at[p], img_s.at[p], img_r.at[p], line(p))
    for p in crossed:
        arrive(pair.at[:, p], fw_s.at[p], pair_r.at[p], (sibling, c))

    def image_ids(shape, axis):
        local = lax.broadcasted_iota(jnp.int32, shape, axis)
        return ((lax.div(local, n) * X + x) * R + r) * n + lax.rem(local, n)

    def pair_ids(shape, axis):
        local = lax.rem(lax.broadcasted_iota(jnp.int32, shape, axis), H)
        block = lax.div(local, n)
        block = lax.div(block, X) * C + a * X + lax.rem(block, X)
        return block * n + lax.rem(local, n)

    images = img[...].reshape(M, F)
    pairs = pair[...].reshape(Q, F)
    s_pi = logit_scale * contract(pairs, images, 1, 1)
    same_pi = image_ids((1, M), 1) == pair_ids((Q, 1), 0)
    diagonal = jnp.sum(jnp.where(same_pi, s_pi, 0.0), axis=0, keepdims=True)
    e_pi = jnp.exp(s_pi - logit_scale)
    text_row = jnp.sum(e_pi[:H], axis=0, keepdims=True)
    audio_row = jnp.sum(e_pi[H:], axis=0, keepdims=True)
    index = lax.broadcasted_iota(jnp.int32, (8, M), 0)
    stat_a[a] = jnp.where(index == 0, text_row, jnp.where(index == 1, audio_row, diagonal))
    for p in lines:
        go(stat_a.at[a], stat_a.at[a], sa_s.at[p], sa_r.at[a], line(p))
    e_ip = jnp.exp(logit_scale * contract(images, pairs, 1, 1) - logit_scale)
    column = jnp.sum(e_ip, axis=0, keepdims=True)
    pieces = [column[:, k : k + 128] for k in range(0, Q, 128)]
    pieces = pieces * max(1, 8 // len(pieces))
    stat_b[b] = jnp.concatenate(pieces, axis=0)
    for p in planes:
        go(stat_b.at[b], stat_b.at[b], sb_s.at[p], sb_r.at[b], plane(p))
    for p in planes:
        arrive(stat_b.at[p], sb_s.at[p], sb_r.at[p], plane(p))
    columns = stat_b[0]
    for p in range(1, B):
        columns = columns + stat_b[p]
    columns = jnp.concatenate([columns[k : k + 1] for k in range(Q // 128)], axis=1)
    inverse_c = 1.0 / columns
    inverse_c_tall = jnp.transpose(jnp.broadcast_to(inverse_c, (128, Q)))
    inverse_c_tall = jnp.concatenate([inverse_c_tall] * (M // 128), axis=1)
    loss_a[a] = jnp.broadcast_to(jnp.sum(jnp.log(columns), keepdims=True), (8, 128))

    for p in lines:
        arrive(stat_a.at[p], sa_s.at[p], sa_r.at[p], line(p))
    totals = stat_a[0]
    for p in range(1, A):
        totals = totals + stat_a[p]
    text_row, audio_row, diagonal = totals[0:1], totals[1:2], totals[2:3]
    loss_part = jnp.sum(jnp.log(text_row) + jnp.log(audio_row) - 2.0 * diagonal, keepdims=True)
    loss_b[b] = jnp.broadcast_to(loss_part, (8, 128))
    inverse_text = jnp.broadcast_to(1.0 / text_row, (H, M))
    inverse_audio = jnp.broadcast_to(1.0 / audio_row, (H, M))
    w_pi = e_pi * (jnp.concatenate([inverse_text, inverse_audio], axis=0) + inverse_c_tall)
    w_pi = (w_pi - jnp.where(same_pi, 2.0, 0.0)).astype(jnp.bfloat16)
    acc[...] = contract(w_pi, images, 1, 0).reshape(2, B, n, F)
    for p in crossed:
        part_p[:, p] = acc[:, p].astype(jnp.bfloat16)
        go(part_p.at[:, p], recv_h.at[:, p], ph_s.at[p], ph_r.at[p], (sibling, c))

    same_ip = image_ids((M, 1), 0) == pair_ids((1, Q), 1)
    inverse_rows = jnp.concatenate(
        [jnp.transpose(inverse_text), jnp.transpose(inverse_audio)], axis=1
    )
    w_ip = e_ip * (inverse_rows + inverse_c)
    w_ip = (w_ip - jnp.where(same_ip, 2.0, 0.0)).astype(jnp.bfloat16)
    part_i[...] = contract(w_ip, pairs, 1, 0).astype(jnp.bfloat16).reshape(A, n, F)
    for p in lines:
        go(part_i.at[p], recv_i.at[a], pi_s.at[p], pi_r.at[a], line(p))
    for p in mates:
        if step == 2:
            arrive(recv_h.at[:, p], ph_s.at[p], ph_r.at[p], (sibling, c))
            part_p[:, p] = (acc[:, p] + recv_h[:, p].astype(jnp.float32)).astype(jnp.bfloat16)
        else:
            part_p[:, p] = acc[:, p].astype(jnp.bfloat16)
        go(part_p.at[:, p], recv_p.at[:, b], pp_s.at[p], pp_r.at[b], plane(p))
    for p in lines:
        go(loss_a.at[a], loss_a.at[a], la_s.at[p], la_r.at[a], line(p))
    for p in planes:
        go(loss_b.at[b], loss_b.at[b], lb_s.at[p], lb_r.at[b], plane(p))

    def finish(values_ref, out_ref, gradient):
        values = values_ref[...].astype(jnp.float32)
        inverse = inverse_radius(values)
        unit = values * inverse
        gradient = logit_scale * gradient
        inner = jnp.sum(unit * gradient, axis=-1, keepdims=True)
        out_ref[...] = (gradient - unit * inner) * inverse

    pair_sum = acc[:, b]
    if step == 2:
        arrive(recv_h.at[:, b], ph_s.at[b], ph_r.at[b], (sibling, c))
        pair_sum = pair_sum + recv_h[:, b].astype(jnp.float32)
    for p in mates[::-1]:
        arrive(recv_p.at[:, p], pp_s.at[p], pp_r.at[p], plane(p))
        pair_sum = pair_sum + recv_p[:, p].astype(jnp.float32)
    finish(text_ref, text_out, pair_sum[0])
    finish(audio_ref, audio_out, pair_sum[1])
    image_sum = part_i[a].astype(jnp.float32)
    for p in lines:
        arrive(recv_i.at[p], pi_s.at[p], pi_r.at[p], line(p))
        image_sum = image_sum + recv_i[p].astype(jnp.float32)
    finish(image_ref, image_out, image_sum)
    for p in lines:
        arrive(loss_a.at[p], la_s.at[p], la_r.at[p], line(p))
    for p in planes:
        arrive(loss_b.at[p], lb_s.at[p], lb_r.at[p], plane(p))
    total = loss_a[0]
    for p in range(1, A):
        total = total + loss_a[p]
    for p in range(B):
        total = total + loss_b[p]
    loss_out[0, 0] = jnp.max(total) / (4.0 * n * R * C) + logit_scale
    for one in sent:
        one.wait_send()


def solution(mesh):
    R, C = mesh.shape["row"], mesh.shape["col"]
    X = 1
    while R * X < C // X and C % (2 * X) == 0:
        X *= 2
    A, B = C // X, R * X

    def shards(image, text, audio):
        n, F = image.shape
        M, Q = A * n, 2 * B * n
        vmem = pl.BlockSpec(memory_space=pltpu.VMEM)
        f32, bf16 = jnp.float32, jnp.bfloat16
        grad = pltpu.VMEM((n, F), f32)
        sem = pltpu.SemaphoreType.DMA
        sems = [sem((A,))] * 8 + [sem((B,))] * 11
        image_grad, text_grad, audio_grad, loss = pl.pallas_call(
            functools.partial(kernel, R, C, X, n, F),
            out_shape=(grad, grad, grad, jax.ShapeDtypeStruct((1, 1), f32)),
            in_specs=[vmem] * 3,
            out_specs=(vmem, vmem, vmem, pl.BlockSpec(memory_space=pltpu.SMEM)),
            scratch_shapes=[
                pltpu.VMEM((A, n, F), bf16),
                pltpu.VMEM((2, B, n, F), bf16),
                pltpu.VMEM((A, 8, M), f32),
                pltpu.VMEM((B, max(8, Q // 128), 128), f32),
                pltpu.VMEM((A, 8, 128), f32),
                pltpu.VMEM((B, 8, 128), f32),
                pltpu.VMEM((A, n, F), bf16),
                pltpu.VMEM((A, n, F), bf16),
                pltpu.VMEM((2, B, n, F), f32),
                pltpu.VMEM((2, B, n, F), bf16),
                pltpu.VMEM((2, B, n, F), bf16),
                pltpu.VMEM((2, B, n, F), bf16),
            ]
            + sems,
            compiler_params=pltpu.CompilerParams(
                collective_id=0, has_side_effects=True, vmem_limit_bytes=48 << 20
            ),
        )(image, text, audio)
        return image_grad, text_grad, audio_grad, loss.reshape(())

    first, second = P(("col", "row"), None), P(("row", "col"), None)
    return jax.shard_map(
        shards,
        mesh=mesh,
        in_specs=(first, second, second),
        out_specs=(first, second, second, P()),
        check_vma=False,
    )
```

time: 185 us -> 37.2 us (0.20)
  blocking collectives: 111 us -> 0 us
  waiting for transfers between devices: 43.2 us -> 0 us
  Pallas kernels: 0 us -> 30.1 us
  between operations: 19.2 us -> 2.39 us
  other arithmetic: 7.92 us -> 0 us
  local copies, waits for them, and re-layouts: 0.02 us -> 4.48 us
  matrix products: 3.67 us -> 0 us
    psum x3 -> x0, blocking collectives: 65.4 us -> none  [the longest x1 37.1 us: shards(): lax.psum(loss_part, ('row', 'col')) / (4.0 * batch_size) + logit_scale]
    all_gather x3 -> x0, blocking collectives: 45.2 us -> none  [the longest x1 32 us: shards(): image_tile = lax.all_gather(image_half, 'col', axis=0, tiled=True)]
    reduce_scatter x2 -> x0, waiting for transfers between devices: 43.2 us -> none  [the longest x1 43.1 us: shards(): lax.psum_scatter(jnp.dot(text_weights, text_tile, preferred_element_type=...]
    pallas_call x0 -> x1, Pallas kernels: none -> 30.1 us  [shards(): pl.pallas_call(functools.partial(kernel, R, C, X, n, F), out_shape=(grad,...]
    unnamed x8 -> x9, local copies, waits for them, and re-layouts: 0.02 us -> 4.48 us
    reduce_sum x7 -> x0, other arithmetic: 3.97 us -> none  [the longest x2 1.39 us: through_norm(): inner = jnp.sum(unit * grad_unit, axis=-1, keepdims=True)]
    dot_general x6 -> x0, matrix products: 3.67 us -> none  [the longest x1 1.35 us: shards(): jnp.dot(audio_weights, audio_tile, preferred_element_type=jnp.float32)]
  transfers between devices with their start and end apart: 2 -> 0, of which waited for: 1 -> 0; matrix products, arithmetic and copies ran while one was open for 3% -> 0% of each run, Pallas kernels for 0% -> 0%
where the time goes in v2:
time: 37.2 us; the launch traced here: 36.9 us
  Pallas kernels  30.1 us (81%)
  local copies, waits for them, and re-layouts  4.48 us (12%)
  between operations  2.39 us (6%)
    pallas_call x1, Pallas kernels, shards(): pl.pallas_call(functools.partial(kernel, R, C, X, n, F), out_shape=(grad,...  30.1 us
    unnamed x9, local copies, waits for them, and re-layouts  4.48 us

profile of v2, /device:TPU:0, one launch (start us, length us, event | category | flops | bytes accessed | tf_op | source)
XLA Modules:
  0.0 36.9 jit_solution(10716810512253158415)
XLA Ops:
  0.6 0.0 copy-start
  0.6 0.8 %copy-done = bf16[32,1024]{1,0:T(8,128)(2,1)S(1)} copy-done((bf16[32,1024]{1,0:T(8,128)(2,1)S(1)}, bf16[32,1024]{1,0:T(8,128)(2,1)}, u32[]{:S(2)}) %copy-start) | copy-done | bytes 65560
  1.5 0.0 copy-start.1
  1.5 0.8 %copy-done.1 = bf16[32,1024]{1,0:T(8,128)(2,1)S(1)} copy-done((bf16[32,1024]{1,0:T(8,128)(2,1)S(1)}, bf16[32,1024]{1,0:T(8,128)(2,1)}, u32[]{:S(2)}) %copy-start.1) | copy-done | bytes 65560
  2.3 0.0 copy-start.2
  2.3 0.8 %copy-done.2 = bf16[32,1024]{1,0:T(8,128)(2,1)S(1)} copy-done((bf16[32,1024]{1,0:T(8,128)(2,1)S(1)}, bf16[32,1024]{1,0:T(8,128)(2,1)}, u32[]{:S(2)}) %copy-start.2) | copy-done | bytes 65560
  3.2 30.1 %shard_map.66 = (f32[32,1024]{1,0:T(8,128)S(1)}, f32[32,1024]{1,0:T(8,128)S(1)}, f32[32,1024]{1,0:T(8,128)S(1)}, f32[1,1]{1,0:T(1,128)}) custom-call(bf16[32,1024]{1,0:T(8,128)(2,1)S(1)} %copy-done, bf16[32,1024]{1,0:T(8,128)(2,1)S(1)} %copy-done.1, bf16[32,1024]{1,0:T(8,128)(2,1)S(1)} %copy-done.2), custom_call_target="tpu_custom_call" | custom-call | tf_op jit(solution)/shard_map/pallas_call | solution.py:234
  33.2 0.7 %copy.11 = f32[32,1024]{1,0:T(8,128)} copy(f32[32,1024]{1,0:T(8,128)S(1)} %get-tuple-element.12) | data formatting | bytes 262144
  33.9 0.7 %copy.12 = f32[32,1024]{1,0:T(8,128)} copy(f32[32,1024]{1,0:T(8,128)S(1)} %get-tuple-element.13) | data formatting | bytes 262144
  34.6 0.7 %copy.13 = f32[32,1024]{1,0:T(8,128)} copy(f32[32,1024]{1,0:T(8,128)S(1)} %get-tuple-element.14) | data formatting | bytes 262144
Async XLA Ops:
  0.6 0.8 %copy-start = (bf16[32,1024]{1,0:T(8,128)(2,1)S(1)}, bf16[32,1024]{1,0:T(8,128)(2,1)}, u32[]{:S(2)}) copy-start(bf16[32,1024]{1,0:T(8,128)(2,1)} %image_ref.1) | copy-start | bytes 196612
  1.5 0.8 %copy-start.1 = (bf16[32,1024]{1,0:T(8,128)(2,1)S(1)}, bf16[32,1024]{1,0:T(8,128)(2,1)}, u32[]{:S(2)}) copy-start(bf16[32,1024]{1,0:T(8,128)(2,1)} %text_ref.1) | copy-start | bytes 196612
  2.3 0.8 %copy-start.2 = (bf16[32,1024]{1,0:T(8,128)(2,1)S(1)}, bf16[32,1024]{1,0:T(8,128)(2,1)}, u32[]{:S(2)}) copy-start(bf16[32,1024]{1,0:T(8,128)(2,1)} %audio_ref.1) | copy-start | bytes 196612

commit v3 on v2

--- a/solution.py
+++ b/solution.py
@@ -24,12 +24,13 @@
 
 def kernel(
     R, C, X, n, F,
-    image_ref, text_ref, audio_ref,
+    image_hbm, text_hbm, audio_hbm,
     image_out, text_out, audio_out, loss_out,
     img, pair, stat_a, stat_b, loss_a, loss_b,
     part_i, recv_i, acc, part_p, recv_h, recv_p,
     img_s, img_r, sa_s, sa_r, la_s, la_r, pi_s, pi_r,
     pair_s, pair_r, sb_s, sb_r, lb_s, lb_r, ph_s, ph_r, pp_s, pp_r, fw_s,
+    image_ref, text_ref, audio_ref, load_s,
 ):
     r = lax.axis_index("row")
     c = lax.axis_index("col")
@@ -79,12 +80,23 @@
     for p in planes:
         pl.semaphore_signal(barrier, inc=1, device_id=plane(p), device_id_type=MESH)
 
+    loads = [
+        pltpu.make_async_copy(src, dst, load_s.at[k])
+        for k, (src, dst) in enumerate(
+            ((text_hbm, text_ref), (audio_hbm, audio_ref), (image_hbm, image_ref))
+        )
+    ]
+    for load in loads:
+        load.start()
+    loads[0].wait()
+    v = text_ref[...].astype(jnp.float32)
+    pair[0, b] = (v * inverse_radius(v)).astype(jnp.bfloat16)
+    loads[1].wait()
+    v = audio_ref[...].astype(jnp.float32)
+    pair[1, b] = (v * inverse_radius(v)).astype(jnp.bfloat16)
+    loads[2].wait()
     v = image_ref[...].astype(jnp.float32)
     img[a] = (v * inverse_radius(v)).astype(jnp.bfloat16)
-    v = text_ref[...].astype(jnp.float32)
-    pair[0, b] = (v * inverse_radius(v)).astype(jnp.bfloat16)
-    v = audio_ref[...].astype(jnp.float32)
-    pair[1, b] = (v * inverse_radius(v)).astype(jnp.bfloat16)
 
     pl.semaphore_wait(barrier, A - 1 + B - 1)
     for p in mates:
@@ -216,6 +228,17 @@
         one.wait_send()
 
 
+def write_back(a_ref, b_ref, c_ref, a_out, b_out, c_out, done):
+    copies = [
+        pltpu.make_async_copy(src, dst, done.at[k])
+        for k, (src, dst) in enumerate(((a_ref, a_out), (b_ref, b_out), (c_ref, c_out)))
+    ]
+    for copy in copies:
+        copy.start()
+    for copy in copies:
+        copy.wait()
+
+
 def solution(mesh):
     R, C = mesh.shape["row"], mesh.shape["col"]
     X = 1
@@ -227,6 +250,7 @@
         n, F = image.shape
         M, Q = A * n, 2 * B * n
         vmem = pl.BlockSpec(memory_space=pltpu.VMEM)
+        hbm = pl.BlockSpec(memory_space=pltpu.HBM)
         f32, bf16 = jnp.float32, jnp.bfloat16
         grad = pltpu.VMEM((n, F), f32)
         sem = pltpu.SemaphoreType.DMA
@@ -234,7 +258,7 @@
         image_grad, text_grad, audio_grad, loss = pl.pallas_call(
             functools.partial(kernel, R, C, X, n, F),
             out_shape=(grad, grad, grad, jax.ShapeDtypeStruct((1, 1), f32)),
-            in_specs=[vmem] * 3,
+            in_specs=[hbm] * 3,
             out_specs=(vmem, vmem, vmem, pl.BlockSpec(memory_space=pltpu.SMEM)),
             scratch_shapes=[
                 pltpu.VMEM((A, n, F), bf16),
@@ -250,11 +274,22 @@
                 pltpu.VMEM((2, B, n, F), bf16),
                 pltpu.VMEM((2, B, n, F), bf16),
             ]
-            + sems,
+            + sems
+            + [pltpu.VMEM((n, F), bf16)] * 3
+            + [sem((3,))],
             compiler_params=pltpu.CompilerParams(
-                collective_id=0, has_side_effects=True, vmem_limit_bytes=48 << 20
+                collective_id=0, has_side_effects=True, vmem_limit_bytes=67043328 - 13 * n * F
             ),
         )(image, text, audio)
+        full = jax.ShapeDtypeStruct((n, F), f32)
+        image_grad, text_grad, audio_grad = pl.pallas_call(
+            write_back,
+            out_shape=(full,) * 3,
+            in_specs=[vmem] * 3,
+            out_specs=(hbm,) * 3,
+            scratch_shapes=[sem((3,))],
+            compiler_params=pltpu.CompilerParams(vmem_limit_bytes=1 << 20),
+        )(image_grad, text_grad, audio_grad)
         return image_grad, text_grad, audio_grad, loss.reshape(())
 
     first, second = P(("col", "row"), None), P(("row", "col"), None)

time: 37.2 us -> 33.6 us (0.903)
  local copies, waits for them, and re-layouts: 4.48 us -> 0 us
  Pallas kernels: 30.1 us -> 31 us
    unnamed x9 -> x0, local copies, waits for them, and re-layouts: 4.48 us -> none
    pallas_call x0 -> x1, Pallas kernels: none -> 0.77 us  [shards(): pl.pallas_call(write_back, out_shape=(full,) * 3, in_specs=[vmem] * 3, ou...]
where the time goes in v3:
time: 33.6 us; the launch traced here: 33.5 us
  Pallas kernels  31 us (92%)
  between operations  2.4 us (7%)
    pallas_call x1, Pallas kernels, shards(): pl.pallas_call(functools.partial(kernel, R, C, X, n, F), out_shape=(grad,...  30.3 us
    pallas_call x1, Pallas kernels, shards(): pl.pallas_call(write_back, out_shape=(full,) * 3, in_specs=[vmem] * 3, ou...  0.77 us

profile of v3, /device:TPU:0, one launch (start us, length us, event | category | flops | bytes accessed | tf_op | source)
XLA Modules:
  0.0 33.5 jit_solution(5189871786058573325)
XLA Ops:
  0.6 30.3 %shard_map.66 = (f32[32,1024]{1,0:T(8,128)S(1)}, f32[32,1024]{1,0:T(8,128)S(1)}, f32[32,1024]{1,0:T(8,128)S(1)}, f32[1,1]{1,0:T(1,128)}) custom-call(bf16[32,1024]{1,0:T(8,128)(2,1)} %image_hbm.1, bf16[32,1024]{1,0:T(8,128)(2,1)} %text_hbm.1, bf16[32,1024]{1,0:T(8,128)(2,1)} %audio_hbm.1), custom_call_target="tpu_custom_call" | custom-call | tf_op jit(solution)/shard_map/pallas_call | solution.py:258
  30.9 0.8 %shard_map.67 = (f32[32,1024]{1,0:T(8,128)}, f32[32,1024]{1,0:T(8,128)}, f32[32,1024]{1,0:T(8,128)}) custom-call(f32[32,1024]{1,0:T(8,128)S(1)} %get-tuple-element.11.a_ref, f32[32,1024]{1,0:T(8,128)S(1)} %get-tuple-element.12.b_ref, f32[32,1024]{1,0:T(8,128)S(1)} %get-tuple-element.13.c_ref), custom_call_target="tpu_custom_call" | custom-call | tf_op jit(solution)/shard_map/pallas_call | solution.py:285

commit v4 on v3

--- a/solution.py
+++ b/solution.py
@@ -42,7 +42,9 @@
     b = r * X + x
     step = 2 if R % 2 == 0 else 1
     sibling = r + 1 - 2 * lax.rem(r, 2)
-    lines = [lax.rem(a + k, A) for k in range(1, A)]
+    side = 2 * lax.rem(a, 2) - 1
+    far_first = sorted(range(1, A), key=lambda k: abs(2 * k - A))
+    lines = [lax.rem(a + side * k + A, A) for k in far_first]
     planes = [lax.rem(b + k, B) for k in range(1, B)]
     turns = [
         (lax.rem(r + i, R), lax.rem(x + j, X))
@@ -153,6 +155,8 @@
     inverse_c_tall = jnp.transpose(jnp.broadcast_to(inverse_c, (128, Q)))
     inverse_c_tall = jnp.concatenate([inverse_c_tall] * (M // 128), axis=1)
     loss_a[a] = jnp.broadcast_to(jnp.sum(jnp.log(columns), keepdims=True), (8, 128))
+    for p in lines:
+        go(loss_a.at[a], loss_a.at[a], la_s.at[p], la_r.at[a], line(p))
 
     for p in lines:
         arrive(stat_a.at[p], sa_s.at[p], sa_r.at[p], line(p))
@@ -162,6 +166,8 @@
     text_row, audio_row, diagonal = totals[0:1], totals[1:2], totals[2:3]
     loss_part = jnp.sum(jnp.log(text_row) + jnp.log(audio_row) - 2.0 * diagonal, keepdims=True)
     loss_b[b] = jnp.broadcast_to(loss_part, (8, 128))
+    for p in planes:
+        go(loss_b.at[b], loss_b.at[b], lb_s.at[p], lb_r.at[b], plane(p))
     inverse_text = jnp.broadcast_to(1.0 / text_row, (H, M))
     inverse_audio = jnp.broadcast_to(1.0 / audio_row, (H, M))
     w_pi = e_pi * (jnp.concatenate([inverse_text, inverse_audio], axis=0) + inverse_c_tall)
@@ -187,10 +193,6 @@
         else:
             part_p[:, p] = acc[:, p].astype(jnp.bfloat16)
         go(part_p.at[:, p], recv_p.at[:, b], pp_s.at[p], pp_r.at[b], plane(p))
-    for p in lines:
-        go(loss_a.at[a], loss_a.at[a], la_s.at[p], la_r.at[a], line(p))
-    for p in planes:
-        go(loss_b.at[b], loss_b.at[b], lb_s.at[p], lb_r.at[b], plane(p))
 
     def finish(values_ref, out_ref, gradient):
         values = values_ref[...].astype(jnp.float32)

time: 33.6 us -> 33.6 us (level)
  no operation moved by 1% of the time
where the time goes in v4:
time: 33.6 us; the launch traced here: 33.4 us
  Pallas kernels  31 us (92%)
  between operations  2.4 us (7%)
    pallas_call x1, Pallas kernels, shards(): pl.pallas_call(functools.partial(kernel, R, C, X, n, F), out_shape=(grad,...  30.2 us
    pallas_call x1, Pallas kernels, shards(): pl.pallas_call(write_back, out_shape=(full,) * 3, in_specs=[vmem] * 3, ou...  0.77 us

profile of v4, /device:TPU:0, one launch (start us, length us, event | category | flops | bytes accessed | tf_op | source)
XLA Modules:
  0.0 33.4 jit_solution(11862215829417204345)
XLA Ops:
  0.6 30.2 %shard_map.66 = (f32[32,1024]{1,0:T(8,128)S(1)}, f32[32,1024]{1,0:T(8,128)S(1)}, f32[32,1024]{1,0:T(8,128)S(1)}, f32[1,1]{1,0:T(1,128)}) custom-call(bf16[32,1024]{1,0:T(8,128)(2,1)} %image_hbm.1, bf16[32,1024]{1,0:T(8,128)(2,1)} %text_hbm.1, bf16[32,1024]{1,0:T(8,128)(2,1)} %audio_hbm.1), custom_call_target="tpu_custom_call" | custom-call | tf_op jit(solution)/shard_map/pallas_call | solution.py:260
  30.9 0.8 %shard_map.67 = (f32[32,1024]{1,0:T(8,128)}, f32[32,1024]{1,0:T(8,128)}, f32[32,1024]{1,0:T(8,128)}) custom-call(f32[32,1024]{1,0:T(8,128)S(1)} %get-tuple-element.11.a_ref, f32[32,1024]{1,0:T(8,128)S(1)} %get-tuple-element.12.b_ref, f32[32,1024]{1,0:T(8,128)S(1)} %get-tuple-element.13.c_ref), custom_call_target="tpu_custom_call" | custom-call | tf_op jit(solution)/shard_map/pallas_call | solution.py:287

commit v5 on v4

--- a/solution.py
+++ b/solution.py
@@ -101,20 +101,26 @@
     img[a] = (v * inverse_radius(v)).astype(jnp.bfloat16)
 
     pl.semaphore_wait(barrier, A - 1 + B - 1)
-    for p in mates:
-        go(pair.at[:, b], pair.at[:, b], pair_s.at[p], pair_r.at[b], plane(p))
+    both = (0, 1)
+    for m in both:
+        for p in mates:
+            go(pair.at[m, b], pair.at[m, b], pair_s.at[m * B + p], pair_r.at[m * B + b], plane(p))
     for p in lines:
         go(img.at[a], img.at[a], img_s.at[p], img_r.at[a], line(p))
     if step == 2:
-        go(pair.at[:, b], pair.at[:, b], fw_s.at[b], pair_r.at[b], (sibling, c))
-    for p in mates[::-1]:
-        arrive(pair.at[:, p], pair_s.at[p], pair_r.at[p], plane(p))
-        if step == 2:
-            go(pair.at[:, p], pair.at[:, p], fw_s.at[p], pair_r.at[p], (sibling, c))
+        for m in both:
+            go(pair.at[m, b], pair.at[m, b], fw_s.at[m * B + b], pair_r.at[m * B + b], (sibling, c))
+    for m in both:
+        for p in mates[::-1]:
+            k = m * B + p
+            arrive(pair.at[m, p], pair_s.at[k], pair_r.at[k], plane(p))
+            if step == 2:
+                go(pair.at[m, p], pair.at[m, p], fw_s.at[k], pair_r.at[k], (sibling, c))
     for p in lines:
         arrive(img.at[p], img_s.at[p], img_r.at[p], line(p))
-    for p in crossed:
-        arrive(pair.at[:, p], fw_s.at[p], pair_r.at[p], (sibling, c))
+    for m in both:
+        for p in crossed:
+            arrive(pair.at[m, p], fw_s.at[m * B + p], pair_r.at[m * B + p], (sibling, c))
 
     def image_ids(shape, axis):
         local = lax.broadcasted_iota(jnp.int32, shape, axis)
@@ -172,10 +178,12 @@
     inverse_audio = jnp.broadcast_to(1.0 / audio_row, (H, M))
     w_pi = e_pi * (jnp.concatenate([inverse_text, inverse_audio], axis=0) + inverse_c_tall)
     w_pi = (w_pi - jnp.where(same_pi, 2.0, 0.0)).astype(jnp.bfloat16)
-    acc[...] = contract(w_pi, images, 1, 0).reshape(2, B, n, F)
-    for p in crossed:
-        part_p[:, p] = acc[:, p].astype(jnp.bfloat16)
-        go(part_p.at[:, p], recv_h.at[:, p], ph_s.at[p], ph_r.at[p], (sibling, c))
+    for m in both:
+        acc[m] = contract(w_pi[m * H : (m + 1) * H], images, 1, 0).reshape(B, n, F)
+        for p in crossed:
+            k = m * B + p
+            part_p[m, p] = acc[m, p].astype(jnp.bfloat16)
+            go(part_p.at[m, p], recv_h.at[m, p], ph_s.at[k], ph_r.at[k], (sibling, c))
 
     same_ip = image_ids((M, 1), 0) == pair_ids((1, Q), 1)
     inverse_rows = jnp.concatenate(
@@ -186,13 +194,15 @@
     part_i[...] = contract(w_ip, pairs, 1, 0).astype(jnp.bfloat16).reshape(A, n, F)
     for p in lines:
         go(part_i.at[p], recv_i.at[a], pi_s.at[p], pi_r.at[a], line(p))
-    for p in mates:
-        if step == 2:
-            arrive(recv_h.at[:, p], ph_s.at[p], ph_r.at[p], (sibling, c))
-            part_p[:, p] = (acc[:, p] + recv_h[:, p].astype(jnp.float32)).astype(jnp.bfloat16)
-        else:
-            part_p[:, p] = acc[:, p].astype(jnp.bfloat16)
-        go(part_p.at[:, p], recv_p.at[:, b], pp_s.at[p], pp_r.at[b], plane(p))
+    for m in both:
+        for p in mates:
+            k = m * B + p
+            partial = acc[m, p]
+            if step == 2:
+                arrive(recv_h.at[m, p], ph_s.at[k], ph_r.at[k], (sibling, c))
+                partial = partial + recv_h[m, p].astype(jnp.float32)
+            part_p[m, p] = partial.astype(jnp.bfloat16)
+            go(part_p.at[m, p], recv_p.at[m, b], pp_s.at[k], pp_r.at[m * B + b], plane(p))
 
     def finish(values_ref, out_ref, gradient):
         values = values_ref[...].astype(jnp.float32)
@@ -202,15 +212,15 @@
         inner = jnp.sum(unit * gradient, axis=-1, keepdims=True)
         out_ref[...] = (gradient - unit * inner) * inverse
 
-    pair_sum = acc[:, b]
-    if step == 2:
-        arrive(recv_h.at[:, b], ph_s.at[b], ph_r.at[b], (sibling, c))
-        pair_sum = pair_sum + recv_h[:, b].astype(jnp.float32)
-    for p in mates[::-1]:
-        arrive(recv_p.at[:, p], pp_s.at[p], pp_r.at[p], plane(p))
-        pair_sum = pair_sum + recv_p[:, p].astype(jnp.float32)
-    finish(text_ref, text_out, pair_sum[0])
-    finish(audio_ref, audio_out, pair_sum[1])
+    for m, values_ref, out_ref in ((0, text_ref, text_out), (1, audio_ref, audio_out)):
+        pair_sum = acc[m, b]
+        if step == 2:
+            arrive(recv_h.at[m, b], ph_s.at[m * B + b], ph_r.at[m * B + b], (sibling, c))
+            pair_sum = pair_sum + recv_h[m, b].astype(jnp.float32)
+        for p in mates[::-1]:
+            arrive(recv_p.at[m, p], pp_s.at[m * B + p], pp_r.at[m * B + p], plane(p))
+            pair_sum = pair_sum + recv_p[m, p].astype(jnp.float32)
+        finish(values_ref, out_ref, pair_sum)
     image_sum = part_i[a].astype(jnp.float32)
     for p in lines:
         arrive(recv_i.at[p], pi_s.at[p], pi_r.at[p], line(p))
@@ -256,7 +266,7 @@
         f32, bf16 = jnp.float32, jnp.bfloat16
         grad = pltpu.VMEM((n, F), f32)
         sem = pltpu.SemaphoreType.DMA
-        sems = [sem((A,))] * 8 + [sem((B,))] * 11
+        sems = [sem((A,))] * 8 + [sem((2 * B,))] * 2 + [sem((B,))] * 4 + [sem((2 * B,))] * 5
         image_grad, text_grad, audio_grad, loss = pl.pallas_call(
             functools.partial(kernel, R, C, X, n, F),
             out_shape=(grad, grad, grad, jax.ShapeDtypeStruct((1, 1), f32)),

time: 33.6 us -> 33.4 us (level)
  no operation moved by 1% of the time
where the time goes in v5:
time: 33.4 us; the launch traced here: 33.3 us
  Pallas kernels  30.9 us (93%)
  between operations  2.4 us (7%)
    pallas_call x1, Pallas kernels, shards(): pl.pallas_call(functools.partial(kernel, R, C, X, n, F), out_shape=(grad,...  30.1 us
    pallas_call x1, Pallas kernels, shards(): pl.pallas_call(write_back, out_shape=(full,) * 3, in_specs=[vmem] * 3, ou...  0.77 us

profile of v5, /device:TPU:0, one launch (start us, length us, event | category | flops | bytes accessed | tf_op | source)
XLA Modules:
  0.0 33.3 jit_solution(422179533359881190)
XLA Ops:
  0.6 30.1 %shard_map.66 = (f32[32,1024]{1,0:T(8,128)S(1)}, f32[32,1024]{1,0:T(8,128)S(1)}, f32[32,1024]{1,0:T(8,128)S(1)}, f32[1,1]{1,0:T(1,128)}) custom-call(bf16[32,1024]{1,0:T(8,128)(2,1)} %image_hbm.1, bf16[32,1024]{1,0:T(8,128)(2,1)} %text_hbm.1, bf16[32,1024]{1,0:T(8,128)(2,1)} %audio_hbm.1), custom_call_target="tpu_custom_call" | custom-call | tf_op jit(solution)/shard_map/pallas_call | solution.py:270
  30.7 0.8 %shard_map.67 = (f32[32,1024]{1,0:T(8,128)}, f32[32,1024]{1,0:T(8,128)}, f32[32,1024]{1,0:T(8,128)}) custom-call(f32[32,1024]{1,0:T(8,128)S(1)} %get-tuple-element.11.a_ref, f32[32,1024]{1,0:T(8,128)S(1)} %get-tuple-element.12.b_ref, f32[32,1024]{1,0:T(8,128)S(1)} %get-tuple-element.13.c_ref), custom_call_target="tpu_custom_call" | custom-call | tf_op jit(solution)/shard_map/pallas_call | solution.py:297

commit v6 on v5

--- a/solution.py
+++ b/solution.py
@@ -178,13 +178,6 @@
     inverse_audio = jnp.broadcast_to(1.0 / audio_row, (H, M))
     w_pi = e_pi * (jnp.concatenate([inverse_text, inverse_audio], axis=0) + inverse_c_tall)
     w_pi = (w_pi - jnp.where(same_pi, 2.0, 0.0)).astype(jnp.bfloat16)
-    for m in both:
-        acc[m] = contract(w_pi[m * H : (m + 1) * H], images, 1, 0).reshape(B, n, F)
-        for p in crossed:
-            k = m * B + p
-            part_p[m, p] = acc[m, p].astype(jnp.bfloat16)
-            go(part_p.at[m, p], recv_h.at[m, p], ph_s.at[k], ph_r.at[k], (sibling, c))
-
     same_ip = image_ids((M, 1), 0) == pair_ids((1, Q), 1)
     inverse_rows = jnp.concatenate(
         [jnp.transpose(inverse_text), jnp.transpose(inverse_audio)], axis=1
@@ -194,6 +187,12 @@
     part_i[...] = contract(w_ip, pairs, 1, 0).astype(jnp.bfloat16).reshape(A, n, F)
     for p in lines:
         go(part_i.at[p], recv_i.at[a], pi_s.at[p], pi_r.at[a], line(p))
+    for m in both:
+        acc[m] = contract(w_pi[m * H : (m + 1) * H], images, 1, 0).reshape(B, n, F)
+        for p in crossed:
+            k = m * B + p
+            part_p[m, p] = acc[m, p].astype(jnp.bfloat16)
+            go(part_p.at[m, p], recv_h.at[m, p], ph_s.at[k], ph_r.at[k], (sibling, c))
     for m in both:
         for p in mates:
             k = m * B + p

time: 33.4 us -> 33.6 us (level)
  no operation moved by 1% of the time
where the time goes in v6:
time: 33.6 us; the launch traced here: 33.4 us
  Pallas kernels  31 us (92%)
  between operations  2.4 us (7%)
    pallas_call x1, Pallas kernels, shards(): pl.pallas_call(functools.partial(kernel, R, C, X, n, F), out_shape=(grad,...  30.3 us
    pallas_call x1, Pallas kernels, shards(): pl.pallas_call(write_back, out_shape=(full,) * 3, in_specs=[vmem] * 3, ou...  0.77 us

profile of v6, /device:TPU:0, one launch (start us, length us, event | category | flops | bytes accessed | tf_op | source)
XLA Modules:
  0.0 33.4 jit_solution(16195518052299173784)
XLA Ops:
  0.6 30.3 %shard_map.66 = (f32[32,1024]{1,0:T(8,128)S(1)}, f32[32,1024]{1,0:T(8,128)S(1)}, f32[32,1024]{1,0:T(8,128)S(1)}, f32[1,1]{1,0:T(1,128)}) custom-call(bf16[32,1024]{1,0:T(8,128)(2,1)} %image_hbm.1, bf16[32,1024]{1,0:T(8,128)(2,1)} %text_hbm.1, bf16[32,1024]{1,0:T(8,128)(2,1)} %audio_hbm.1), custom_call_target="tpu_custom_call" | custom-call | tf_op jit(solution)/shard_map/pallas_call | solution.py:269
  30.9 0.8 %shard_map.67 = (f32[32,1024]{1,0:T(8,128)}, f32[32,1024]{1,0:T(8,128)}, f32[32,1024]{1,0:T(8,128)}) custom-call(f32[32,1024]{1,0:T(8,128)S(1)} %get-tuple-element.11.a_ref, f32[32,1024]{1,0:T(8,128)S(1)} %get-tuple-element.12.b_ref, f32[32,1024]{1,0:T(8,128)S(1)} %get-tuple-element.13.c_ref), custom_call_target="tpu_custom_call" | custom-call | tf_op jit(solution)/shard_map/pallas_call | solution.py:296
